TPU v7x, 32 devices: a whole 2x2x4 slice. The times are simulated.
32 devices in a mesh: blk: 4 (over y, core), group: 8 (over z, x).
Axes of the slice: x: 2, y: 2, z: 4, core: 2. Of those that a mesh axis runs over, the one named last changes fastest.
Arguments:
- queries: bfloat16 [32, 16, 128], P(('blk', 'group')), may hold values from -2.5 to 2.5
- query_mask: int32 [32, 16], P(('blk', 'group')), may hold values from 0 to 1, as said below
- positive: int32 [32], P(('blk', 'group')), may hold values from 0 to 63
- page_vectors: bfloat16 [64, 128, 128], P(('blk', 'group')), may hold values from -2 to 2
- page_mask: int32 [64, 128], P(('blk', 'group')), may hold values from 0 to 1, as said below
Outputs:
- grad_queries: float32 [32, 16, 128], P(('blk', 'group'))
- grad_pages: float32 [64, 128, 128], P(('blk', 'group'))
- mean_loss: float32 [], replicated
Inputs may be any that keep to these rules, and one draw needn't show every extreme that they name: `query_mask`: each row holds ones on its first 8 to 16 token slots and zeros after them. `page_mask`: each row holds ones on its first 32 to 128 patch slots and zeros after them.
All inputs are finite; a program needn't handle non-finite values.
Results may differ from a plain program's by a relative error of at most 0.0028.
Values may be sent and summed in bfloat16 or wider, within the bound.
No kernel may reach another device: no remote copies, remote signals or barrier semaphores. Data moves between devices by JAX's collectives and lax.ppermute only.
A program may use at most 64 MiB of HBM per device.

v0:
```python
import math
import jax
import jax.numpy as jnp
from jax import lax
from jax.sharding import PartitionSpec as P

relaxation_scale_factor = 0.5
guarded_floor_entry = -1e30


def combined_all(part, axis, combine):
    gathered = jax.tree.map(lambda a: lax.all_gather(a, axis), part)

    def take(source):
        return jax.tree.map(lambda a: lax.dynamic_index_in_dim(a, source, 0, False), gathered)

    return lax.fori_loop(
        1, lax.axis_size(axis), lambda source, state: combine(state, take(source)), take(0)
    )


def from_behind(value, axis, steps):
    count = lax.axis_size(axis)
    pairs = [(source, (source + steps) % count) for source in range(count)]
    return lax.ppermute(value, axis, pairs)


def masked_logits(row_block, lone_document, live_image_embeddings):
    similarity_matrix = lax.dot_general(
        row_block, lone_document, (((1,), (1,)), ((), ())), preferred_element_type=jnp.float32
    )
    return jnp.where(
        live_image_embeddings[None, :] > 0,
        similarity_matrix / relaxation_scale_factor,
        guarded_floor_entry,
    )


def combine_parts(earlier, later):
    highest = jnp.maximum(earlier[0], later[0])
    totals = earlier[1] * jnp.exp(earlier[0] - highest) + later[1] * jnp.exp(later[0] - highest)
    return (highest, totals, earlier[2] + later[2])


def on_device(queries, query_mask, positive, page_vectors, page_mask):
    tokens = queries.shape[1]
    features = queries.shape[2]
    local_pages = page_vectors.shape[0]
    blocks = lax.axis_size("blk")
    members = lax.axis_size("group")
    bundle_size = queries.shape[0] * members
    total_queries = bundle_size * blocks
    natural_logarithm_lengths = jnp.log(jnp.sum(page_mask.astype(jnp.float32), axis=1))
    bundle_vectors, bundle_masks, bundle_targets = (
        lax.all_gather(queries, "group", axis=0, tiled=True),
        lax.all_gather(query_mask, "group", axis=0, tiled=True),
        lax.all_gather(positive, "group", axis=0, tiled=True),
    )

    def forward_piece(folded, shard_in, root_row):
        scores, lse_rows, live_all, owners, kept = folded
        vectors, token_masks, targets = shard_in
        amount = vectors.shape[0]
        stride = math.gcd(amount, max(1, 512 // tokens))

        def run_block(number, current):
            scores, lse_rows = current
            offset = number * stride
            slab_rows = lax.dynamic_slice_in_dim(vectors, offset, stride, 0).reshape(
                stride * tokens, features
            )
            alive = lax.dynamic_slice_in_dim(token_masks, offset, stride, 0).astype(jnp.float32)
            found_sums = []
            for index_page in range(local_pages):
                masked = masked_logits(slab_rows, page_vectors[index_page], page_mask[index_page])
                highest = jnp.max(masked, axis=1, keepdims=True)
                found_sums.append(
                    highest[:, 0] + jnp.log(jnp.sum(jnp.exp(masked - highest), axis=1))
                )
            logsumexp_results = jnp.stack(found_sums, axis=1).reshape(stride, tokens, local_pages)
            softened_supremum = relaxation_scale_factor * (
                logsumexp_results - natural_logarithm_lengths
            )
            page_score = jnp.sum(alive[:, :, None] * softened_supremum, axis=1)
            scores = lax.dynamic_update_slice_in_dim(scores, page_score, offset, 0)
            lse_rows = lax.dynamic_update_slice_in_dim(lse_rows, logsumexp_results, offset, 0)
            return (scores, lse_rows)

        scores, lse_rows = lax.fori_loop(0, amount // stride, run_block, (scores, lse_rows))
        live_all = lax.dynamic_update_slice_in_dim(live_all, token_masks, root_row, 0)
        owners = lax.dynamic_update_slice_in_dim(owners, targets, root_row, 0)
        kept = vectors
        return (scores, lse_rows, live_all, owners, kept)

    starting = (
        jnp.zeros((total_queries, local_pages), jnp.float32),
        jnp.zeros((total_queries, tokens, local_pages), jnp.float32),
        jnp.zeros((total_queries, tokens), jnp.int32),
        jnp.zeros((total_queries,), jnp.int32),
        jnp.zeros((total_queries, tokens, features), jnp.bfloat16),
    )
    scores, lse_rows, live_all, owners, kept = forward_piece(
        starting,
        (
            lax.all_gather(bundle_vectors, "blk", axis=0, tiled=True),
            lax.all_gather(bundle_masks, "blk", axis=0, tiled=True),
            lax.all_gather(bundle_targets, "blk", axis=0, tiled=True),
        ),
        jnp.int32(0),
    )
    position = lax.axis_index(("blk", "group"))
    page_ids = position * local_pages + jnp.arange(local_pages, dtype=jnp.int32)
    chosen = owners[:, None] == page_ids[None, :]
    picked_local = jnp.sum(jnp.where(chosen, scores, 0.0))
    local_top = jnp.max(scores, axis=1)
    local_total = jnp.sum(jnp.exp(scores - local_top[:, None]), axis=1)
    highest, totals, picked = combined_all(
        (local_top, local_total, picked_local), ("blk", "group"), combine_parts
    )
    page_lse = highest + jnp.log(totals)
    mean_loss = (jnp.sum(page_lse) - picked) / total_queries
    coefficient = jnp.exp(scores - page_lse[:, None]) - chosen.astype(jnp.float32)
    factor_scale = coefficient[:, None, :] * live_all.astype(jnp.float32)[:, :, None]

    def slice_rows(root_row, amount):
        sums = lax.dynamic_slice_in_dim(lse_rows, root_row, amount, 0).reshape(
            amount * tokens, local_pages
        )
        scales = lax.dynamic_slice_in_dim(factor_scale, root_row, amount, 0).reshape(
            amount * tokens, local_pages
        )
        return (sums, scales)

    def gradient_terms(row_block, logsumexp_results, scales, page_grads):
        partial_value = jnp.zeros(row_block.shape, jnp.float32)
        for number in range(local_pages):
            masked = masked_logits(row_block, page_vectors[number], page_mask[number])
            weights = jnp.exp(masked - logsumexp_results[:, number : number + 1])
            factor = (scales[:, number : number + 1] * weights).astype(jnp.bfloat16)
            partial_value = partial_value + jnp.dot(
                factor, page_vectors[number], preferred_element_type=jnp.float32
            )
            update = lax.dot_general(
                factor, row_block, (((0,), (0,)), ((), ())), preferred_element_type=jnp.float32
            )
            page_grads = page_grads.at[number].add(update)
        return (partial_value, page_grads)

    home = lax.axis_index("blk")
    page_grads = jnp.zeros(page_vectors.shape, jnp.float32)

    def visit_one(moving, collected, page_grads, lap_index):
        root_row = (home - lap_index) % blocks * bundle_size
        sums, scales = slice_rows(root_row, bundle_size)
        partial_value, page_grads = gradient_terms(
            moving.reshape(bundle_size * tokens, features), sums, scales, page_grads
        )
        return (collected + partial_value.reshape(bundle_size, tokens, features), page_grads)

    def pass_one(collected):
        return from_behind(collected, "blk", 1)

    def turn_one(lap_index, current):
        moving, collected, page_grads = current
        collected, page_grads = visit_one(moving, collected, page_grads, lap_index)
        moving = from_behind(moving, "blk", 1)
        return (moving, pass_one(collected), page_grads)

    empty_whole = jnp.zeros((bundle_size, tokens, features), jnp.float32)
    moving, collected, page_grads = lax.fori_loop(
        0, blocks - 1, turn_one, (bundle_vectors, empty_whole, page_grads)
    )
    collected, page_grads = visit_one(moving, collected, page_grads, blocks - 1)
    collected = pass_one(collected)
    grad_queries = lax.psum_scatter(collected, "group", scatter_dimension=0, tiled=True)
    return (grad_queries, page_grads, mean_loss)


def solution(mesh):
    in_specs = (
        P(("blk", "group"), None, None),
        P(("blk", "group"), None),
        P(("blk", "group")),
        P(("blk", "group"), None, None),
        P(("blk", "group"), None),
    )
    out_specs = (P(("blk", "group"), None, None), P(("blk", "group"), None, None), P())
    return jax.shard_map(
        on_device, mesh=mesh, in_specs=in_specs, out_specs=out_specs, check_vma=False
    )
```

profile of v0, /device:TPU:0, one launch (start us, length us, event | category | flops | bytes accessed | tf_op | source)
XLA Modules:
  0.0 262.9 jit_solution(15310981650806206361)
XLA Ops:
  7.2 0.8 compare_bitcast_fusion.2
  8.1 32.4 %all_gather.36 = bf16[8,16,128]{2,1,0:T(8,128)(2,1)S(1)} all-gather(bf16[1,16,128]{2,1,0:T(8,128)(2,1)S(1)} %copy-done.4), channel_id=1, replica_groups=mesh['blk'=4,'group'=8] {'group'}, dimensions={0}, use_global_device_ids=true | all-gather | bytes 36864 | tf_op jit(solution)/shard_map/all_gather | solution.py:55
  40.6 5.5 %all_gather.37 = bf16[32,16,128]{2,1,0:T(8,128)(2,1)S(1)} all-gather(bf16[8,16,128]{2,1,0:T(8,128)(2,1)S(1)} %all_gather.36), channel_id=1, replica_groups=mesh['blk'=4,'group'=8] {'blk'}, dimensions={0}, use_global_device_ids=true | all-gather | bytes 163840 | tf_op jit(solution)/shard_map/all_gather | solution.py:105
  46.8 0.7 copy-done.5
  47.5 20.4 %all-gather.2 = s32[8,1,16]{2,1,0:T(1,128)S(1)} all-gather(s32[1,1,16]{2,1,0:T(1,128)S(1)} %bitcast.182), channel_id=1, replica_groups=mesh['blk'=4,'group'=8] {'group'}, dimensions={0}, use_global_device_ids=true | all-gather | bytes 576 | tf_op jit(solution)/shard_map/all_gather | solution.py:56
  67.9 5.2 %all_gather.39 = s32[32,16]{1,0:T(8,128)S(1)} all-gather(s32[8,16]{1,0:T(8,128)S(1)} %bitcast.181), channel_id=1, replica_groups=mesh['blk'=4,'group'=8] {'blk'}, dimensions={0}, use_global_device_ids=true | all-gather | bytes 2560 | tf_op jit(solution)/shard_map/all_gather | solution.py:106
  73.1 0.7 copy-done.7
  75.0 0.8 dynamic-update-slice.28
  75.8 6.8 %all-reduce.2 = s32[8]{0:T(128)S(1)} all-reduce(s32[8]{0:T(128)S(1)} %dynamic-update-slice.28), channel_id=1, replica_groups=mesh['blk'=4,'group'=8] {'group'}, use_global_device_ids=true, to_apply=%add.2 | all-reduce | flops 8 | bytes 64
  84.1 4.9 %all-reduce.3 = s32[32]{0:T(128)S(1)} all-reduce(s32[32]{0:T(128)S(1)} %dynamic-update-slice.29), channel_id=1, replica_groups=mesh['blk'=4,'group'=8] {'blk'}, use_global_device_ids=true, to_apply=%add.3 | all-reduce | flops 32 | bytes 256
  89.2 0.7 fusion.54
  90.3 0.8 dynamic-update-slice.30
  91.0 40.5 %all-reduce.5 = (f32[1024]{0:T(1024)S(1)}, f32[1024]{0:T(1024)S(1)}, f32[32]{0:T(128)S(1)}) all-reduce(f32[1024]{0:T(1024)S(1)} %dynamic-update-slice.26, f32[1024]{0:T(1024)S(1)} %dynamic-update-slice.27, f32[32]{0:T(128)S(1)} %dynamic-update-slice.30), channel_id=2, replica_groups=mesh['blk'=4,'group'=8] {'blk','group'}, use_global_device_ids=true, to_apply=%add | all-reduce | flops 2080 | bytes 16640
  131.7 39.9 %while.48 = (s32[]{:T(128)}, f32[32]{0:T(128)S(1)}, f32[32]{0:T(128)S(1)}, f32[]{:T(128)}, f32[32,32]{1,0:T(8,128)S(1)}, /*index=5*/f32[32,32]{1,0:T(8,128)S(1)}, f32[32]{0:T(128)S(1)}, s32[]{:T(128)}, s32[]{:T(128)}, s32[]{:T(128)}) while((s32[]{:T(128)}, f32[32]{0:T(128)S(1)}, f32[32]{0:T(128)S(1)}, f32[]{:T(128)}, ...), condition=%wide.region_10.11_spmd, body=%wide.region_9.10_spmd.sunk | while | flops 198 | bytes 939 | solution.py:17
  131.7 0.6 dynamic_slice.91
  133.0 0.6 dynamic_slice.91
  134.3 0.6 dynamic_slice.91
  135.6 0.6 dynamic_slice.91
  145.9 0.6 dynamic_slice.91
  147.2 0.6 dynamic_slice.91
  170.4 0.6 dynamic_slice.91
  171.6 0.6 fusion.56
  172.6 13.9 %while.49 = (s32[]{:T(128)}, bf16[8,16,128]{2,1,0:T(8,128)(2,1)S(1)}, f32[8,16,128]{2,1,0:T(8,128)S(1)}, f32[2,128,128]{2,1,0:T(8,128)S(1)}, s32[]{:T(128)}, /*i...) while((s32[]{:T(128)}, ...), condition=%wide.region_12.13_spmd, body=%wide.region_11.12_spmd.sunk | while | flops 25395472 | bytes 1589896 | solution.py:170
  173.6 2.4 collective-permute-start.1
  176.4 0.9 collective-permute-done.1
  178.2 2.4 collective-permute-start.1
  181.0 0.9 collective-permute-done.1
  182.8 2.4 collective-permute-start.1
  185.6 0.9 collective-permute-done.1
  188.1 2.8 %collective-permute-done.2 = f32[8,16,128]{2,1,0:T(8,128)S(1)} collective-permute-done((f32[8,16,128]{2,1,0:T(8,128)S(1)}, f32[8,16,128]{2,1,0:T(8,128)S(1)}, u32[]{:S(2)}, u32[]{:S(2)}) %collective-permute-start.2) | collective-permute-done | bytes 65568 | tf_op jit(solution)/shard_map/ppermute | solution.py:25
  190.9 0.6 copy-done.2
  191.8 63.1 %reduce-scatter.2.cloned.1.call-done = f32[1,16,128]{2,1,0:T(8,128)} async-done(((f32[8,16,128]{2,1,0:T(8,128)}), f32[1,16,128]{2,1,0:T(8,128)}) %reduce-scatter.2.cloned.1.call-update) | async-done | bytes 8208 | tf_op jit(solution)/shard_map/reduce_scatter | solution.py:175
  (166 shorter events, 23.0 us)
Async XLA Ops:
  7.2 0.8 copy-start.3
  7.2 0.9 copy-start.4
  7.2 247.7 %reduce-scatter.2.cloned.1.call-start = ((), (), s32[]{:S(2)}) async-start(), calls=%async_computation.1 | async-start | bytes 73728 | tf_op jit(solution)/shard_map/reduce_scatter | solution.py:175
  40.5 5.5 %copy-start.1 = (bf16[2,128,128]{2,1,0:T(8,128)(2,1)S(1)}, bf16[2,128,128]{2,1,0:T(8,128)(2,1)}, u32[]{:S(2)}) copy-start(bf16[2,128,128]{2,1,0:T(8,128)(2,1)} %param.20) | copy-start | bytes 196612
  46.8 0.7 copy-start.5
  73.1 0.7 copy-start.7
  75.8 6.8 %copy-start.6 = (u32[32]{0:T(128)S(1)}, u32[32]{0:T(128)}, u32[]{:S(2)}) copy-start(u32[32]{0:T(128)} %constant.385) | copy-start | bytes 388
  172.6 3.7 %collective-permute-start = (bf16[8,16,128]{2,1,0:T(8,128)(2,1)S(1)}, bf16[8,16,128]{2,1,0:T(8,128)(2,1)S(1)}, u32[]{:S(2)}, u32[]{:S(2)}) collective-permute-start(bf16[8,16,128]{2,1,0:T(8,128)(2,1)S(1)} %copy.33), channel_id=1, source_target_pairs={{0,8},{8,16},{16,24},{24,0},{1,9},{9,17},{17,25},{25,1},{2,10},{10... | collective-permute-start | bytes 98312 | tf_op jit(solution)/shard_map/while/body/eval_jaxpr/ppermute | solution.py:25
  173.6 3.7 %collective-permute-start.1 = (f32[8,16,128]{2,1,0:T(8,128)S(1)}, f32[8,16,128]{2,1,0:T(8,128)S(1)}, u32[]{:S(2)}, u32[]{:S(2)}) collective-permute-start(f32[8,16,128]{2,1,0:T(8,128)S(1)} %add.305), channel_id=1, source_target_pairs={{0,8},{8,16},{16,24},{24,0},{1,9},{9,17},{17,25},{25,1},{2,10},{10... | collective-permute-start | bytes 196616 | tf_op jit(solution)/shard_map/while/body/eval_jaxpr/ppermute | solution.py:25
  177.3 3.7 %collective-permute-start = (bf16[8,16,128]{2,1,0:T(8,128)(2,1)S(1)}, bf16[8,16,128]{2,1,0:T(8,128)(2,1)S(1)}, u32[]{:S(2)}, u32[]{:S(2)}) collective-permute-start(bf16[8,16,128]{2,1,0:T(8,128)(2,1)S(1)} %copy.33), channel_id=1, source_target_pairs={{0,8},{8,16},{16,24},{24,0},{1,9},{9,17},{17,25},{25,1},{2,10},{10... | collective-permute-start | bytes 98312 | tf_op jit(solution)/shard_map/while/body/eval_jaxpr/ppermute | solution.py:25
  178.2 3.7 %collective-permute-start.1 = (f32[8,16,128]{2,1,0:T(8,128)S(1)}, f32[8,16,128]{2,1,0:T(8,128)S(1)}, u32[]{:S(2)}, u32[]{:S(2)}) collective-permute-start(f32[8,16,128]{2,1,0:T(8,128)S(1)} %add.305), channel_id=1, source_target_pairs={{0,8},{8,16},{16,24},{24,0},{1,9},{9,17},{17,25},{25,1},{2,10},{10... | collective-permute-start | bytes 196616 | tf_op jit(solution)/shard_map/while/body/eval_jaxpr/ppermute | solution.py:25
  182.0 3.6 %collective-permute-start = (bf16[8,16,128]{2,1,0:T(8,128)(2,1)S(1)}, bf16[8,16,128]{2,1,0:T(8,128)(2,1)S(1)}, u32[]{:S(2)}, u32[]{:S(2)}) collective-permute-start(bf16[8,16,128]{2,1,0:T(8,128)(2,1)S(1)} %copy.33), channel_id=1, source_target_pairs={{0,8},{8,16},{16,24},{24,0},{1,9},{9,17},{17,25},{25,1},{2,10},{10... | collective-permute-start | bytes 98312 | tf_op jit(solution)/shard_map/while/body/eval_jaxpr/ppermute | solution.py:25
  182.8 3.7 %collective-permute-start.1 = (f32[8,16,128]{2,1,0:T(8,128)S(1)}, f32[8,16,128]{2,1,0:T(8,128)S(1)}, u32[]{:S(2)}, u32[]{:S(2)}) collective-permute-start(f32[8,16,128]{2,1,0:T(8,128)S(1)} %add.305), channel_id=1, source_target_pairs={{0,8},{8,16},{16,24},{24,0},{1,9},{9,17},{17,25},{25,1},{2,10},{10... | collective-permute-start | bytes 196616 | tf_op jit(solution)/shard_map/while/body/eval_jaxpr/ppermute | solution.py:25
  187.2 3.7 %collective-permute-start.2 = (f32[8,16,128]{2,1,0:T(8,128)S(1)}, f32[8,16,128]{2,1,0:T(8,128)S(1)}, u32[]{:S(2)}, u32[]{:S(2)}) collective-permute-start(f32[8,16,128]{2,1,0:T(8,128)S(1)} %add.250), channel_id=1, source_target_pairs={{0,8},{8,16},{16,24},{24,0},{1,9},{9,17},{17,25},{25,1},{2,10},{10... | collective-permute-start | bytes 196616 | tf_op jit(solution)/shard_map/ppermute | solution.py:25
  190.9 0.6 copy-start.2
  191.8 63.1 %copy-start = (f32[2,128,128]{2,1,0:T(8,128)}, f32[2,128,128]{2,1,0:T(8,128)S(1)}, u32[]{:S(2)}) copy-start(f32[2,128,128]{2,1,0:T(8,128)S(1)} %fusion.38) | copy-start | bytes 393220
Sparse Core Ops, SparseCore 0:
  191.7 63.1 reduce-scatter.1
where the time goes:
time: 264 us; the launch traced here: 263 us
  blocking collectives  116 us (44%)
  waiting for transfers between devices  68.8 us (26%)
  local copies, waits for them, and re-layouts  24.5 us (9%)
  loops' own time  21.1 us (8%)
  between operations  17.3 us (7%)
  starting transfers between devices  7.44 us (3%)
  matrix products  4.3 us (2%)
  other arithmetic  3.58 us (1%)
    reduce_scatter x1, waiting for transfers between devices, on_device(): lax.psum_scatter(collected, 'group', scatter_dimension=0, tiled=True)  63.1 us
    unnamed x3, blocking collectives  52.2 us
    all_gather x1, blocking collectives, on_device(): lax.all_gather(queries, 'group', axis=0, tiled=True)  32.4 us
    another operation x1, loops' own time, combined_all(): lax.fori_loop(1, lax.axis_size(axis), lambda source, state: combine(state...  20.9 us
    all_gather x1, blocking collectives, on_device(): lax.all_gather(query_mask, 'group', axis=0, tiled=True)  20.4 us
    dynamic_slice x33, local copies, waits for them, and re-layouts, take(): lax.dynamic_index_in_dim(a, source, 0, False)  18.2 us
    ppermute x7, starting transfers between devices, from_behind(): return lax.ppermute(value, axis, pairs)  7.4 us
    ppermute x7, waiting for transfers between devices, from_behind(): return lax.ppermute(value, axis, pairs)  5.66 us
  transfers between devices with their start and end apart: 8, of which 5 were waited for; matrix products, arithmetic and copies ran while one was open for 1% of the time, Pallas kernels for 0%

commit v1 on v0

--- a/solution.py
+++ b/solution.py
@@ -6,6 +6,28 @@
 
 relaxation_scale_factor = 0.5
 guarded_floor_entry = -1e30
+
+
+def laid_out(blocks, dim):
+    blocks = jnp.moveaxis(blocks, 0, dim)
+    lengths = blocks.shape
+    return blocks.reshape(*lengths[:dim], lengths[dim] * lengths[dim + 1], *lengths[dim + 2 :])
+
+
+def doubled(array, axis):
+    count = lax.axis_size(axis)
+    parts = array[None]
+    for level in range(count.bit_length() - 1):
+        distance = 1 << level
+        other = lax.ppermute(parts, axis, [(i, i ^ distance) for i in range(count)])
+        both = jnp.stack([parts, other])
+        upper = lax.axis_index(axis) >> level & 1
+        parts = jnp.where(upper == 0, both, both[::-1]).reshape(-1, *array.shape)
+    return parts
+
+
+def doubled_up(x, axis, dim):
+    return laid_out(doubled(x, axis), dim)
 
 
 def combined_all(part, axis, combine):
@@ -53,7 +75,7 @@
     natural_logarithm_lengths = jnp.log(jnp.sum(page_mask.astype(jnp.float32), axis=1))
     bundle_vectors, bundle_masks, bundle_targets = (
         lax.all_gather(queries, "group", axis=0, tiled=True),
-        lax.all_gather(query_mask, "group", axis=0, tiled=True),
+        doubled_up(query_mask, "group", 0),
         lax.all_gather(positive, "group", axis=0, tiled=True),
     )
 

time: 264 us -> 249 us (0.943)
  blocking collectives: 116 us -> 94.8 us
  starting transfers between devices: 7.44 us -> 13 us
    all_gather x1 -> x0, blocking collectives: 20.4 us -> none  [on_device(): lax.all_gather(query_mask, 'group', axis=0, tiled=True)]
    ppermute x0 -> x3, starting transfers between devices: none -> 5.58 us  [doubled(): other = lax.ppermute(parts, axis, [(i, i ^ distance) for i in range(count)])]
  transfers between devices with their start and end apart: 8 -> 11, of which waited for: 5 -> 5; matrix products, arithmetic and copies ran while one was open for 1% -> 3% of each run, Pallas kernels for 0% -> 0%
where the time goes in v1:
time: 249 us; the launch traced here: 248 us
  blocking collectives  94.8 us (38%)
  waiting for transfers between devices  69 us (28%)
  local copies, waits for them, and re-layouts  25.2 us (10%)
  loops' own time  21.1 us (8%)
  between operations  17.3 us (7%)
  starting transfers between devices  13 us (5%)
  matrix products  4.3 us (2%)
  other arithmetic  3 us (1%)
    reduce_scatter x1, waiting for transfers between devices, on_device(): lax.psum_scatter(collected, 'group', scatter_dimension=0, tiled=True)  63.4 us
    unnamed x3, blocking collectives  53.2 us
    all_gather x1, blocking collectives, on_device(): lax.all_gather(queries, 'group', axis=0, tiled=True)  30.9 us
    another operation x1, loops' own time, combined_all(): lax.fori_loop(1, lax.axis_size(axis), lambda source, state: combine(state...  20.9 us
    dynamic_slice x33, local copies, waits for them, and re-layouts, take(): lax.dynamic_index_in_dim(a, source, 0, False)  18.2 us
    ppermute x7, starting transfers between devices, from_behind(): return lax.ppermute(value, axis, pairs)  7.4 us
    unnamed x29, local copies, waits for them, and re-layouts  5.99 us
    ppermute x7, waiting for transfers between devices, from_behind(): return lax.ppermute(value, axis, pairs)  5.66 us
  transfers between devices with their start and end apart: 11, of which 5 were waited for; matrix products, arithmetic and copies ran while one was open for 3% of the time, Pallas kernels for 0%

profile of v1, /device:TPU:0, one launch (start us, length us, event | category | flops | bytes accessed | tf_op | source)
XLA Modules:
  0.0 247.9 jit_solution(8727537257648169158)
XLA Ops:
  7.2 0.6 copy-done.5
  7.8 3.0 %collective-permute-start.2 = (s32[1,1,16]{2,1,0:T(1,128)S(1)}, s32[1,1,16]{2,1,0:T(1,128)S(1)}, u32[]{:S(2)}, u32[]{:S(2)}) collective-permute-start(s32[1,1,16]{2,1,0:T(1,128)S(1)} %bitcast.196), channel_id=1, source_target_pairs={{0,1},{1,0},{2,3},{3,2},{4,5},{5,4},{6,7},{7,6},{8,9},{9,8},{10,11... | collective-permute-start | bytes 200 | tf_op jit(solution)/shard_map/ppermute | solution.py:22
  11.0 0.7 copy-done.4
  11.6 30.9 %all_gather.33 = bf16[8,16,128]{2,1,0:T(8,128)(2,1)S(1)} all-gather(bf16[1,16,128]{2,1,0:T(8,128)(2,1)S(1)} %copy-done.4), channel_id=1, replica_groups=mesh['blk'=4,'group'=8] {'group'}, dimensions={0}, use_global_device_ids=true | all-gather | bytes 36864 | tf_op jit(solution)/shard_map/all_gather | solution.py:77
  42.6 5.5 %all_gather.34 = bf16[32,16,128]{2,1,0:T(8,128)(2,1)S(1)} all-gather(bf16[8,16,128]{2,1,0:T(8,128)(2,1)S(1)} %all_gather.33), channel_id=1, replica_groups=mesh['blk'=4,'group'=8] {'blk'}, dimensions={0}, use_global_device_ids=true | all-gather | bytes 163840 | tf_op jit(solution)/shard_map/all_gather | solution.py:127
  48.9 0.6 copy-done.7
  49.5 0.7 dynamic-slice.50
  51.5 0.8 dynamic-update-slice.28
  52.9 10.0 %all-reduce.2 = s32[8]{0:T(128)S(1)} all-reduce(s32[8]{0:T(128)S(1)} %dynamic-update-slice.28), channel_id=1, replica_groups=mesh['blk'=4,'group'=8] {'group'}, use_global_device_ids=true, to_apply=%add.2 | all-reduce | flops 8 | bytes 64
  62.9 2.5 %collective-permute-start.4 = (s32[4,1,16]{2,0,1:T(4,128)S(1)}, s32[4,1,16]{2,0,1:T(4,128)S(1)}, u32[]{:S(2)}, u32[]{:S(2)}) collective-permute-start(s32[4,1,16]{2,0,1:T(4,128)S(1)} %bitcast.190), channel_id=1, source_target_pairs={{0,4},{1,5},{2,6},{3,7},{4,0},{5,1},{6,2},{7,3},{8,12},{9,13},{10,... | collective-permute-start | bytes 776 | tf_op jit(solution)/shard_map/ppermute | solution.py:22
  65.6 4.9 %all-reduce.3 = s32[32]{0:T(128)S(1)} all-reduce(s32[32]{0:T(128)S(1)} %dynamic-update-slice.29), channel_id=1, replica_groups=mesh['blk'=4,'group'=8] {'blk'}, use_global_device_ids=true, to_apply=%add.3 | all-reduce | flops 32 | bytes 256
  70.6 5.2 %all_gather.35 = s32[32,16]{1,0:T(8,128)S(1)} all-gather(s32[8,16]{1,0:T(8,128)S(1)} %bitcast.189), channel_id=1, replica_groups=mesh['blk'=4,'group'=8] {'blk'}, dimensions={0}, use_global_device_ids=true | all-gather | bytes 2560 | tf_op jit(solution)/shard_map/all_gather | solution.py:128
  76.0 0.8 fusion.54
  77.1 0.8 dynamic-update-slice.30
  77.9 38.3 %all-reduce.5 = (f32[1024]{0:T(1024)S(1)}, f32[1024]{0:T(1024)S(1)}, f32[32]{0:T(128)S(1)}) all-reduce(f32[1024]{0:T(1024)S(1)} %dynamic-update-slice.26, f32[1024]{0:T(1024)S(1)} %dynamic-update-slice.27, f32[32]{0:T(128)S(1)} %dynamic-update-slice.30), channel_id=2, replica_groups=mesh['blk'=4,'group'=8] {'blk','group'}, use_global_device_ids=true, to_apply=%add | all-reduce | flops 2080 | bytes 16640
  116.4 40.0 %while.48 = (s32[]{:T(128)}, f32[32]{0:T(128)S(1)}, f32[32]{0:T(128)S(1)}, f32[]{:T(128)}, f32[32,32]{1,0:T(8,128)S(1)}, /*index=5*/f32[32,32]{1,0:T(8,128)S(1)}, f32[32]{0:T(128)S(1)}, s32[]{:T(128)}, s32[]{:T(128)}, s32[]{:T(128)}) while((s32[]{:T(128)}, f32[32]{0:T(128)S(1)}, f32[32]{0:T(128)S(1)}, f32[]{:T(128)}, ...), condition=%wide.region_10.11_spmd, body=%wide.region_9.10_spmd.sunk | while | flops 198 | bytes 939 | solution.py:39
  116.4 0.6 dynamic_slice.91
  117.7 0.6 dynamic_slice.91
  120.3 0.6 dynamic_slice.91
  141.0 0.6 dynamic_slice.91
  144.8 0.6 dynamic_slice.91
  156.4 0.6 fusion.56
  157.4 13.9 %while.49 = (s32[]{:T(128)}, bf16[8,16,128]{2,1,0:T(8,128)(2,1)S(1)}, f32[8,16,128]{2,1,0:T(8,128)S(1)}, f32[2,128,128]{2,1,0:T(8,128)S(1)}, s32[]{:T(128)}, /*i...) while((s32[]{:T(128)}, ...), condition=%wide.region_12.13_spmd, body=%wide.region_11.12_spmd.sunk | while | flops 25395472 | bytes 1589896 | solution.py:192
  158.3 2.4 collective-permute-start.1
  161.1 0.9 collective-permute-done.1
  163.0 2.4 collective-permute-start.1
  165.8 0.9 collective-permute-done.1
  167.6 2.4 collective-permute-start.1
  170.4 0.9 collective-permute-done.1
  172.9 2.8 %collective-permute-done.5 = f32[8,16,128]{2,1,0:T(8,128)S(1)} collective-permute-done((f32[8,16,128]{2,1,0:T(8,128)S(1)}, f32[8,16,128]{2,1,0:T(8,128)S(1)}, u32[]{:S(2)}, u32[]{:S(2)}) %collective-permute-start.5) | collective-permute-done | bytes 65568 | tf_op jit(solution)/shard_map/ppermute | solution.py:47
  175.7 0.6 copy-done.2
  176.5 63.4 %reduce-scatter.2.cloned.1.call-done = f32[1,16,128]{2,1,0:T(8,128)} async-done(((f32[8,16,128]{2,1,0:T(8,128)}), f32[1,16,128]{2,1,0:T(8,128)}) %reduce-scatter.2.cloned.1.call-update) | async-done | bytes 8208 | tf_op jit(solution)/shard_map/reduce_scatter | solution.py:197
  (177 shorter events, 23.8 us)
Async XLA Ops:
  7.2 0.7 copy-start.5
  7.2 232.7 %reduce-scatter.2.cloned.1.call-start = ((), (), s32[]{:S(2)}) async-start(), calls=%async_computation.1 | async-start | bytes 73728 | tf_op jit(solution)/shard_map/reduce_scatter | solution.py:197
  7.8 3.0 %copy-start.3 = (s32[2,128]{1,0:T(2,128)S(1)}, s32[2,128]{1,0:T(2,128)}, u32[]{:S(2)}) copy-start(s32[2,128]{1,0:T(2,128)} %param.21) | copy-start | bytes 3076
  7.8 44.4 %collective-permute-start.2 = (s32[1,1,16]{2,1,0:T(1,128)S(1)}, s32[1,1,16]{2,1,0:T(1,128)S(1)}, u32[]{:S(2)}, u32[]{:S(2)}) collective-permute-start(s32[1,1,16]{2,1,0:T(1,128)S(1)} %bitcast.196), channel_id=1, source_target_pairs={{0,1},{1,0},{2,3},{3,2},{4,5},{5,4},{6,7},{7,6},{8,9},{9,8},{10,11... | collective-permute-start | bytes 200 | tf_op jit(solution)/shard_map/ppermute | solution.py:22
  10.9 0.7 copy-start.4
  42.6 5.5 %copy-start.1 = (bf16[2,128,128]{2,1,0:T(8,128)(2,1)S(1)}, bf16[2,128,128]{2,1,0:T(8,128)(2,1)}, u32[]{:S(2)}) copy-start(bf16[2,128,128]{2,1,0:T(8,128)(2,1)} %param.20) | copy-start | bytes 196612
  48.9 0.7 copy-start.7
  50.2 0.7 copy-start.6
  52.3 10.6 %collective-permute-start.3 = (s32[2,1,16]{2,0,1:T(2,128)S(1)}, s32[2,1,16]{2,0,1:T(2,128)S(1)}, u32[]{:S(2)}, u32[]{:S(2)}) collective-permute-start(s32[2,1,16]{2,0,1:T(2,128)S(1)} %bitcast.192), channel_id=1, source_target_pairs={{0,2},{1,3},{2,0},{3,1},{4,6},{5,7},{6,4},{7,5},{8,10},{9,11},{10,... | collective-permute-start | bytes 392 | tf_op jit(solution)/shard_map/ppermute | solution.py:22
  62.9 7.7 %collective-permute-start.4 = (s32[4,1,16]{2,0,1:T(4,128)S(1)}, s32[4,1,16]{2,0,1:T(4,128)S(1)}, u32[]{:S(2)}, u32[]{:S(2)}) collective-permute-start(s32[4,1,16]{2,0,1:T(4,128)S(1)} %bitcast.190), channel_id=1, source_target_pairs={{0,4},{1,5},{2,6},{3,7},{4,0},{5,1},{6,2},{7,3},{8,12},{9,13},{10,... | collective-permute-start | bytes 776 | tf_op jit(solution)/shard_map/ppermute | solution.py:22
  157.4 3.7 %collective-permute-start = (bf16[8,16,128]{2,1,0:T(8,128)(2,1)S(1)}, bf16[8,16,128]{2,1,0:T(8,128)(2,1)S(1)}, u32[]{:S(2)}, u32[]{:S(2)}) collective-permute-start(bf16[8,16,128]{2,1,0:T(8,128)(2,1)S(1)} %copy.33), channel_id=1, source_target_pairs={{0,8},{8,16},{16,24},{24,0},{1,9},{9,17},{17,25},{25,1},{2,10},{10... | collective-permute-start | bytes 98312 | tf_op jit(solution)/shard_map/while/body/eval_jaxpr/ppermute | solution.py:47
  158.3 3.7 %collective-permute-start.1 = (f32[8,16,128]{2,1,0:T(8,128)S(1)}, f32[8,16,128]{2,1,0:T(8,128)S(1)}, u32[]{:S(2)}, u32[]{:S(2)}) collective-permute-start(f32[8,16,128]{2,1,0:T(8,128)S(1)} %add.311), channel_id=1, source_target_pairs={{0,8},{8,16},{16,24},{24,0},{1,9},{9,17},{17,25},{25,1},{2,10},{10... | collective-permute-start | bytes 196616 | tf_op jit(solution)/shard_map/while/body/eval_jaxpr/ppermute | solution.py:47
  162.1 3.7 %collective-permute-start = (bf16[8,16,128]{2,1,0:T(8,128)(2,1)S(1)}, bf16[8,16,128]{2,1,0:T(8,128)(2,1)S(1)}, u32[]{:S(2)}, u32[]{:S(2)}) collective-permute-start(bf16[8,16,128]{2,1,0:T(8,128)(2,1)S(1)} %copy.33), channel_id=1, source_target_pairs={{0,8},{8,16},{16,24},{24,0},{1,9},{9,17},{17,25},{25,1},{2,10},{10... | collective-permute-start | bytes 98312 | tf_op jit(solution)/shard_map/while/body/eval_jaxpr/ppermute | solution.py:47
  163.0 3.7 %collective-permute-start.1 = (f32[8,16,128]{2,1,0:T(8,128)S(1)}, f32[8,16,128]{2,1,0:T(8,128)S(1)}, u32[]{:S(2)}, u32[]{:S(2)}) collective-permute-start(f32[8,16,128]{2,1,0:T(8,128)S(1)} %add.311), channel_id=1, source_target_pairs={{0,8},{8,16},{16,24},{24,0},{1,9},{9,17},{17,25},{25,1},{2,10},{10... | collective-permute-start | bytes 196616 | tf_op jit(solution)/shard_map/while/body/eval_jaxpr/ppermute | solution.py:47
  166.7 3.6 %collective-permute-start = (bf16[8,16,128]{2,1,0:T(8,128)(2,1)S(1)}, bf16[8,16,128]{2,1,0:T(8,128)(2,1)S(1)}, u32[]{:S(2)}, u32[]{:S(2)}) collective-permute-start(bf16[8,16,128]{2,1,0:T(8,128)(2,1)S(1)} %copy.33), channel_id=1, source_target_pairs={{0,8},{8,16},{16,24},{24,0},{1,9},{9,17},{17,25},{25,1},{2,10},{10... | collective-permute-start | bytes 98312 | tf_op jit(solution)/shard_map/while/body/eval_jaxpr/ppermute | solution.py:47
  167.6 3.7 %collective-permute-start.1 = (f32[8,16,128]{2,1,0:T(8,128)S(1)}, f32[8,16,128]{2,1,0:T(8,128)S(1)}, u32[]{:S(2)}, u32[]{:S(2)}) collective-permute-start(f32[8,16,128]{2,1,0:T(8,128)S(1)} %add.311), channel_id=1, source_target_pairs={{0,8},{8,16},{16,24},{24,0},{1,9},{9,17},{17,25},{25,1},{2,10},{10... | collective-permute-start | bytes 196616 | tf_op jit(solution)/shard_map/while/body/eval_jaxpr/ppermute | solution.py:47
  171.9 3.7 %collective-permute-start.5 = (f32[8,16,128]{2,1,0:T(8,128)S(1)}, f32[8,16,128]{2,1,0:T(8,128)S(1)}, u32[]{:S(2)}, u32[]{:S(2)}) collective-permute-start(f32[8,16,128]{2,1,0:T(8,128)S(1)} %add.250), channel_id=1, source_target_pairs={{0,8},{8,16},{16,24},{24,0},{1,9},{9,17},{17,25},{25,1},{2,10},{10... | collective-permute-start | bytes 196616 | tf_op jit(solution)/shard_map/ppermute | solution.py:47
  175.7 0.6 copy-start.2
  176.5 63.4 %copy-start = (f32[2,128,128]{2,1,0:T(8,128)}, f32[2,128,128]{2,1,0:T(8,128)S(1)}, u32[]{:S(2)}) copy-start(f32[2,128,128]{2,1,0:T(8,128)S(1)} %fusion.38) | copy-start | bytes 393220
Sparse Core Ops, SparseCore 0:
  176.5 63.3 reduce-scatter.1
